TPU v7x, 32 devices: a whole 2x2x4 slice. The times are simulated.
32 devices in a mesh: layer: 16 (over z, x, core), row: 2 (over y).
Axes of the slice: x: 2, y: 2, z: 4, core: 2. Of those that a mesh axis runs over, the one named last changes fastest.
Arguments:
- waves: bfloat16 [16, 3072, 512], P('layer', 'row'), may hold values from -6 to 6
- operators: bfloat16 [16, 4, 3072, 3072], P('layer', None, 'row'), may hold values from -0.0546875 to 0.0546875
- sources: bfloat16 [3072, 512], P('row'), may hold values from -6 to 6
- source_layer: int32 [128], replicated, may hold values from 0 to 15
Outputs:
- traces: bfloat16 [16, 3072, 512], P('layer', 'row')
All inputs are finite; a program needn't handle non-finite values.
Results may differ from a plain program's by a relative error of at most 0.0057.
Values may be sent and summed in bfloat16 or wider, within the bound.
A program may use at most 128 MiB of HBM per device.

v0:
```python
import jax
import jax.numpy as jnp
from jax import lax
from jax.sharding import PartitionSpec as P

TICKS = 3


def shifted(array, axis, by):
    peers = lax.axis_size(axis)
    pairs = [(i, i + by) for i in range(peers) if 0 <= i + by < peers]
    return lax.ppermute(array, axis, pairs)


def combine(real_prod, imag_prod, shot_count):
    real_part = real_prod[:, :shot_count] - imag_prod[:, shot_count:]
    imag_part = real_prod[:, shot_count:] + imag_prod[:, :shot_count]
    return jnp.concatenate([real_part, imag_part], axis=1)


def per_device(waves, operators, sources, source_layer):
    tile_rows = operators.shape[2]
    full_rows = operators.shape[3]
    column_count = waves.shape[2]
    shot_count = column_count // 4
    half = 2 * shot_count
    stacked = operators[0].reshape(4 * tile_rows, full_rows)
    layer_id = lax.axis_index("layer")
    shot_mask = jnp.tile((source_layer == layer_id).astype(jnp.float32), 4)
    source_term = sources.astype(jnp.float32) * shot_mask[None, :]
    current = waves[0]
    for sweep_tick in range(TICKS):
        products = jnp.dot(
            stacked,
            lax.all_gather(current, "row", axis=0, tiled=True),
            preferred_element_type=jnp.float32,
        )
        products = products.reshape(4, tile_rows, column_count)
        down_out = combine(products[0][:, :half], products[1][:, :half], shot_count) + combine(
            products[2][:, half:], products[3][:, half:], shot_count
        )
        up_out = combine(products[0][:, half:], products[1][:, half:], shot_count) + combine(
            products[2][:, :half], products[3][:, :half], shot_count
        )
        down_out = (down_out + source_term[:, :half]).astype(jnp.bfloat16)
        up_out = (up_out + source_term[:, half:]).astype(jnp.bfloat16)
        down_next = shifted(down_out, "layer", 1)
        up_next = shifted(up_out, "layer", -1)
        current = jnp.concatenate([down_next, up_next], axis=1)
    return current[None]


def solution(mesh):
    return jax.shard_map(
        per_device,
        mesh=mesh,
        in_specs=(P("layer", "row", None), P("layer", None, "row", None), P("row", None), P()),
        out_specs=P("layer", "row", None),
        check_vma=False,
    )
```

profile of v0, /device:TPU:9, one launch (start us, length us, event | category | flops | bytes accessed | tf_op | source)
XLA Modules:
  0.0 324.4 jit_solution(11651561303536006612)
XLA Ops:
  7.9 1.6 copy.5
  9.5 1.7 convert_multiply_fusion
  11.2 43.6 %all-gather.9.cloned.1.call-done = bf16[1,3072,512]{2,1,0:T(8,128)(2,1)} async-done(((bf16[1,1536,512]{2,1,0:T(8,128)(2,1)}), bf16[1,3072,512]{2,1,0:T(8,128)(2,1)}) %all-gather.9.cloned.1.call-update) | async-done | bytes 3145744 | tf_op jit(solution)/shard_map/all_gather | solution.py:35
  54.8 26.8 %fusion = f32[6144,512]{0,1:T(8,128)} fusion(bf16[6144,3072]{1,0:T(8,128)(2,1)} %bitcast.17, bf16[1,3072,512]{2,1,0:T(8,128)(2,1)} %all-gather.9.cloned.1.call-done), kind=kOutput, calls=%fused_computation.2 | convolution fusion | flops 19327352832 | bytes 53477376 | tf_op jit(solution)/shard_map/dot_general | solution.py:33
  81.6 6.0 %slice_subtract_fusion.10 = (f32[1536,128]{0,1:T(8,128)S(1)}, f32[1536,128]{0,1:T(8,128)S(1)}, f32[1536,128]{0,1:T(8,128)S(1)}, f32[1536,128]{0,1:T(8,128)S(1)},...) fusion(f32[6144,512]{0,1:T(8,128)} %fusion), kind=kLoop, calls=%fused_computation.47 | loop fusion | flops 1572864 | bytes 18874368 | tf_op jit(solution)/shard_map/sub | solution.py:16
  88.7 3.8 %collective-permute-start = (bf16[1536,256]{0,1:T(8,128)(2,1)S(1)}, bf16[1536,256]{0,1:T(8,128)(2,1)S(1)}, u32[]{:S(2)}, u32[]{:S(2)}) collective-permute-start(bf16[1536,256]{0,1:T(8,128)(2,1)S(1)} %get-tuple-element.33), channel_id=1, source_target_pairs={{0,2},{2,4},{4,6},{6,8},{8,10},{10,12},{12,14},{14,16},{16,18},{18... | collective-permute-start | bytes 2359304 | tf_op jit(solution)/shard_map/ppermute | solution.py:12
  92.5 1.9 collective-permute-start.1
  94.5 15.4 %collective-permute-done = bf16[1536,256]{0,1:T(8,128)(2,1)S(1)} collective-permute-done((bf16[1536,256]{0,1:T(8,128)(2,1)S(1)}, bf16[1536,256]{0,1:T(8,128)(2,1)S(1)}, u32[]{:S(2)}, u32[]{:S(2)}) %collective-permute-start) | collective-permute-done | bytes 786464 | tf_op jit(solution)/shard_map/ppermute | solution.py:12
  109.9 1.6 collective-permute-done.1
  113.0 43.2 %all-gather.5.cloned.1.call-done = bf16[3072,512]{0,1:T(8,128)(2,1)} async-done(((bf16[1536,512]{0,1:T(8,128)(2,1)}), bf16[3072,512]{0,1:T(8,128)(2,1)}) %all-gather.5.cloned.1.call-update) | async-done | bytes 3145744 | tf_op jit(solution)/shard_map/all_gather | solution.py:35
  156.3 27.7 %convolution_bitcast_fusion.1 = f32[6144,512]{0,1:T(8,128)} fusion(bf16[3072,512]{0,1:T(8,128)(2,1)} %all-gather.5.cloned.1.call-done, bf16[6144,3072]{1,0:T(8,128)(2,1)} %bitcast.18), kind=kOutput, calls=%fused_computation.1 | convolution fusion | flops 19327352832 | bytes 53477376 | tf_op jit(solution)/shard_map/dot_general | solution.py:33
  184.0 6.0 %slice_subtract_fusion.6 = (f32[1536,128]{0,1:T(8,128)S(1)}, f32[1536,128]{0,1:T(8,128)S(1)}, f32[1536,128]{0,1:T(8,128)S(1)}, f32[1536,128]{0,1:T(8,128)S(1)}, ...) fusion(f32[6144,512]{0,1:T(8,128)} %convolution_bitcast_fusion.1), kind=kLoop, calls=%fused_computation.39 | loop fusion | flops 1572864 | bytes 18874368 | tf_op jit(solution)/shard_map/sub | solution.py:16
  191.1 3.8 %collective-permute-start.2 = (bf16[1536,256]{0,1:T(8,128)(2,1)S(1)}, bf16[1536,256]{0,1:T(8,128)(2,1)S(1)}, u32[]{:S(2)}, u32[]{:S(2)}) collective-permute-start(bf16[1536,256]{0,1:T(8,128)(2,1)S(1)} %get-tuple-element.31), channel_id=1, source_target_pairs={{0,2},{2,4},{4,6},{6,8},{8,10},{10,12},{12,14},{14,16},{16,18},{18... | collective-permute-start | bytes 2359304 | tf_op jit(solution)/shard_map/ppermute | solution.py:12
  194.9 2.1 collective-permute-start.3
  197.1 15.2 %collective-permute-done.2 = bf16[1536,256]{0,1:T(8,128)(2,1)S(1)} collective-permute-done((bf16[1536,256]{0,1:T(8,128)(2,1)S(1)}, bf16[1536,256]{0,1:T(8,128)(2,1)S(1)}, u32[]{:S(2)}, u32[]{:S(2)}) %collective-permute-start.2) | collective-permute-done | bytes 786464 | tf_op jit(solution)/shard_map/ppermute | solution.py:12
  212.3 1.6 collective-permute-done.3
  215.1 43.5 %all-gather.7.cloned.1.call-done = bf16[3072,512]{0,1:T(8,128)(2,1)} async-done(((bf16[1536,512]{0,1:T(8,128)(2,1)}), bf16[3072,512]{0,1:T(8,128)(2,1)}) %all-gather.7.cloned.1.call-update) | async-done | bytes 3145744 | tf_op jit(solution)/shard_map/all_gather | solution.py:35
  258.6 27.7 %convolution_bitcast_fusion = f32[6144,512]{0,1:T(8,128)} fusion(bf16[3072,512]{0,1:T(8,128)(2,1)} %all-gather.7.cloned.1.call-done, bf16[6144,3072]{1,0:T(8,128)(2,1)} %bitcast.19), kind=kOutput, calls=%fused_computation | convolution fusion | flops 19327352832 | bytes 53477376 | tf_op jit(solution)/shard_map/dot_general | solution.py:33
  286.3 6.0 %slice_subtract_fusion.2 = (f32[1536,128]{0,1:T(8,128)S(1)}, f32[1536,128]{0,1:T(8,128)S(1)}, f32[1536,128]{0,1:T(8,128)S(1)}, f32[1536,128]{0,1:T(8,128)S(1)}, ...) fusion(f32[6144,512]{0,1:T(8,128)} %convolution_bitcast_fusion), kind=kLoop, calls=%fused_computation.31 | loop fusion | flops 1572864 | bytes 18874368 | tf_op jit(solution)/shard_map/sub | solution.py:16
  293.4 3.8 %collective-permute-start.4 = (bf16[1536,256]{0,1:T(8,128)(2,1)S(1)}, bf16[1536,256]{0,1:T(8,128)(2,1)S(1)}, u32[]{:S(2)}, u32[]{:S(2)}) collective-permute-start(bf16[1536,256]{0,1:T(8,128)(2,1)S(1)} %get-tuple-element.29), channel_id=1, source_target_pairs={{0,2},{2,4},{4,6},{6,8},{8,10},{10,12},{12,14},{14,16},{16,18},{18... | collective-permute-start | bytes 2359304 | tf_op jit(solution)/shard_map/ppermute | solution.py:12
  297.3 1.9 collective-permute-start.5
  299.2 15.4 %collective-permute-done.4 = bf16[1536,256]{0,1:T(8,128)(2,1)S(1)} collective-permute-done((bf16[1536,256]{0,1:T(8,128)(2,1)S(1)}, bf16[1536,256]{0,1:T(8,128)(2,1)S(1)}, u32[]{:S(2)}, u32[]{:S(2)}) %collective-permute-start.4) | collective-permute-done | bytes 786464 | tf_op jit(solution)/shard_map/ppermute | solution.py:12
  314.6 1.6 collective-permute-done.5
  316.3 1.6 copy.6
  (18 shorter events, 7.6 us)
Async XLA Ops:
  6.5 1.4 copy-start
  6.5 48.3 %all-gather.9.cloned.1.call-start = ((), (), s32[]{:S(2)}) async-start(), calls=%async_computation.2 | async-start | bytes 4718592 | tf_op jit(solution)/shard_map/all_gather | solution.py:35
  7.3 149.0 %all-gather.5.cloned.1.call-start = ((), (), s32[]{:S(2)}) async-start(), calls=%async_computation | async-start | bytes 4718592 | tf_op jit(solution)/shard_map/all_gather | solution.py:35
  7.9 1.6 copy-start.1
  88.7 21.2 %collective-permute-start = (bf16[1536,256]{0,1:T(8,128)(2,1)S(1)}, bf16[1536,256]{0,1:T(8,128)(2,1)S(1)}, u32[]{:S(2)}, u32[]{:S(2)}) collective-permute-start(bf16[1536,256]{0,1:T(8,128)(2,1)S(1)} %get-tuple-element.33), channel_id=1, source_target_pairs={{0,2},{2,4},{4,6},{6,8},{8,10},{10,12},{12,14},{14,16},{16,18},{18... | collective-permute-start | bytes 2359304 | tf_op jit(solution)/shard_map/ppermute | solution.py:12
  92.5 19.0 %collective-permute-start.1 = (bf16[1536,256]{0,1:T(8,128)(2,1)S(1)}, bf16[1536,256]{0,1:T(8,128)(2,1)S(1)}, u32[]{:S(2)}, u32[]{:S(2)}) collective-permute-start(bf16[1536,256]{0,1:T(8,128)(2,1)S(1)} %get-tuple-element.34), channel_id=1, source_target_pairs={{2,0},{4,2},{6,4},{8,6},{10,8},{12,10},{14,12},{16,14},{18,16},{20... | collective-permute-start | bytes 2359304 | tf_op jit(solution)/shard_map/ppermute | solution.py:12
  112.8 145.8 %all-gather.7.cloned.1.call-start = ((), (), s32[]{:S(2)}) async-start(), calls=%async_computation.1 | async-start | bytes 4718592 | tf_op jit(solution)/shard_map/all_gather | solution.py:35
  191.1 21.2 %collective-permute-start.2 = (bf16[1536,256]{0,1:T(8,128)(2,1)S(1)}, bf16[1536,256]{0,1:T(8,128)(2,1)S(1)}, u32[]{:S(2)}, u32[]{:S(2)}) collective-permute-start(bf16[1536,256]{0,1:T(8,128)(2,1)S(1)} %get-tuple-element.31), channel_id=1, source_target_pairs={{0,2},{2,4},{4,6},{6,8},{8,10},{10,12},{12,14},{14,16},{16,18},{18... | collective-permute-start | bytes 2359304 | tf_op jit(solution)/shard_map/ppermute | solution.py:12
  194.9 19.0 %collective-permute-start.3 = (bf16[1536,256]{0,1:T(8,128)(2,1)S(1)}, bf16[1536,256]{0,1:T(8,128)(2,1)S(1)}, u32[]{:S(2)}, u32[]{:S(2)}) collective-permute-start(bf16[1536,256]{0,1:T(8,128)(2,1)S(1)} %get-tuple-element.32), channel_id=1, source_target_pairs={{2,0},{4,2},{6,4},{8,6},{10,8},{12,10},{14,12},{16,14},{18,16},{20... | collective-permute-start | bytes 2359304 | tf_op jit(solution)/shard_map/ppermute | solution.py:12
  293.4 21.2 %collective-permute-start.4 = (bf16[1536,256]{0,1:T(8,128)(2,1)S(1)}, bf16[1536,256]{0,1:T(8,128)(2,1)S(1)}, u32[]{:S(2)}, u32[]{:S(2)}) collective-permute-start(bf16[1536,256]{0,1:T(8,128)(2,1)S(1)} %get-tuple-element.29), channel_id=1, source_target_pairs={{0,2},{2,4},{4,6},{6,8},{8,10},{10,12},{12,14},{14,16},{16,18},{18... | collective-permute-start | bytes 2359304 | tf_op jit(solution)/shard_map/ppermute | solution.py:12
  297.3 19.0 %collective-permute-start.5 = (bf16[1536,256]{0,1:T(8,128)(2,1)S(1)}, bf16[1536,256]{0,1:T(8,128)(2,1)S(1)}, u32[]{:S(2)}, u32[]{:S(2)}) collective-permute-start(bf16[1536,256]{0,1:T(8,128)(2,1)S(1)} %get-tuple-element.30), channel_id=1, source_target_pairs={{2,0},{4,2},{6,4},{8,6},{10,8},{12,10},{14,12},{16,14},{18,16},{20... | collective-permute-start | bytes 2359304 | tf_op jit(solution)/shard_map/ppermute | solution.py:12
Sparse Core Ops, SparseCore 0:
  8.9 45.8 all-gather.8
  112.9 43.3 all-gather.4
  215.3 43.3 all-gather.6
where the time goes:
time: 325 us; the launch traced here: 324 us
  waiting for transfers between devices  182 us (56%)
  matrix products  82.2 us (25%)
  other arithmetic  25.6 us (8%)
  starting transfers between devices  17.7 us (5%)
  between operations  13.2 us (4%)
  local copies, waits for them, and re-layouts  3.78 us (1%)
    all_gather x3, waiting for transfers between devices, per_device(): lax.all_gather(current, 'row', axis=0, tiled=True)  130 us
    dot_general x3, matrix products, per_device(): jnp.dot(stacked, lax.all_gather(current, 'row', axis=0, tiled=True), pref...  82.2 us
    ppermute x6, waiting for transfers between devices, shifted(): return lax.ppermute(array, axis, pairs)  50.9 us
    sub x3, other arithmetic, combine(): real_part = real_prod[:, :shot_count] - imag_prod[:, shot_count:]  17.9 us
    ppermute x6, starting transfers between devices, shifted(): return lax.ppermute(array, axis, pairs)  17.4 us
  transfers between devices with their start and end apart: 9, of which 9 were waited for; matrix products, arithmetic and copies ran while one was open for 1% of the time, Pallas kernels for 0%

commit v1 on v0

--- a/solution.py
+++ b/solution.py
@@ -32,7 +32,12 @@
     for sweep_tick in range(TICKS):
         products = jnp.dot(
             stacked,
-            lax.all_gather(current, "row", axis=0, tiled=True),
+            jnp.concatenate(
+                lax.all_to_all(
+                    jnp.stack([current for _ in range(lax.axis_size("row"))]), "row", 0, 0
+                ),
+                axis=0,
+            ),
             preferred_element_type=jnp.float32,
         )
         products = products.reshape(4, tile_rows, column_count)

time: 325 us -> 296 us (0.911)
  waiting for transfers between devices: 182 us -> 80.1 us
  blocking collectives: 0 us -> 66.8 us
  between operations: 13.2 us -> 0.14 us
  local copies, waits for them, and re-layouts: 3.78 us -> 12.6 us
  starting transfers between devices: 17.7 us -> 24.9 us
    all_gather x3 -> x0, waiting for transfers between devices: 130 us -> none  [per_device(): lax.all_gather(current, 'row', axis=0, tiled=True)]
    all_to_all x0 -> x2, blocking collectives: none -> 66.8 us  [per_device(): lax.all_to_all(jnp.stack([current for _ in range(lax.axis_size('row'))]),...]
    all_to_all x0 -> x1, waiting for transfers between devices: none -> 32.3 us  [per_device(): lax.all_to_all(jnp.stack([current for _ in range(lax.axis_size('row'))]),...]
    all_to_all x0 -> x2, local copies, waits for them, and re-layouts: none -> 9.48 us  [per_device(): lax.all_to_all(jnp.stack([current for _ in range(lax.axis_size('row'))]),...]
    all_to_all x0 -> x1, starting transfers between devices: none -> 5.35 us  [per_device(): lax.all_to_all(jnp.stack([current for _ in range(lax.axis_size('row'))]),...]
    another operation x0 -> x5, other arithmetic: none -> 4.56 us  [per_device(): jnp.stack([current for _ in range(lax.axis_size('row'))])]
  transfers between devices with their start and end apart: 9 -> 7, of which waited for: 9 -> 5; matrix products, arithmetic and copies ran while one was open for 1% -> 1% of each run, Pallas kernels for 0% -> 0%
where the time goes in v1:
time: 296 us; the launch traced here: 295 us
  matrix products  82.8 us (28%)
  waiting for transfers between devices  80.1 us (27%)
  blocking collectives  66.8 us (23%)
  other arithmetic  27.7 us (9%)
  starting transfers between devices  24.9 us (8%)
  local copies, waits for them, and re-layouts  12.6 us (4%)
    dot_general x3, matrix products, per_device(): jnp.dot(stacked, jnp.concatenate(lax.all_to_all(jnp.stack([current for _...  82.8 us
    all_to_all x2, blocking collectives, per_device(): lax.all_to_all(jnp.stack([current for _ in range(lax.axis_size('row'))]),...  66.8 us
    ppermute x6, waiting for transfers between devices, shifted(): return lax.ppermute(array, axis, pairs)  47.8 us
    all_to_all x1, waiting for transfers between devices, per_device(): lax.all_to_all(jnp.stack([current for _ in range(lax.axis_size('row'))]),...  32.3 us
    ppermute x6, starting transfers between devices, shifted(): return lax.ppermute(array, axis, pairs)  19.5 us
    sub x3, other arithmetic, combine(): real_part = real_prod[:, :shot_count] - imag_prod[:, shot_count:]  17.9 us
    all_to_all x2, local copies, waits for them, and re-layouts, per_device(): lax.all_to_all(jnp.stack([current for _ in range(lax.axis_size('row'))]),...  9.48 us
  transfers between devices with their start and end apart: 7, of which 5 were waited for; matrix products, arithmetic and copies ran while one was open for 1% of the time, Pallas kernels for 0%

profile of v1, /device:TPU:9, one launch (start us, length us, event | category | flops | bytes accessed | tf_op | source)
XLA Modules:
  0.0 295.0 jit_solution(1667937115095855908)
XLA Ops:
  0.0 3.8 %pad_maximum_fusion = bf16[2,1536,512]{2,1,0:T(8,128)(2,1)} fusion(bf16[1,1536,512]{2,1,0:T(8,128)(2,1)} %param.4), kind=kLoop, calls=%fused_computation.3 | loop fusion | flops 1572864 | bytes 4718592 | tf_op jit(solution)/shard_map/stack | solution.py:37
  3.8 5.4 %all-to-all-start = ((bf16[2,1536,512]{2,1,0:T(8,128)(2,1)}), bf16[2,1536,512]{2,1,0:T(8,128)(2,1)}, u32[]{:S(2)}, u32[]{:S(2)}) async-start(bf16[2,1536,512]{2,1,0:T(8,128)(2,1)} %pad_maximum_fusion), calls=%async_computation | async-start | bytes 6291456 | tf_op jit(solution)/shard_map/all_to_all | solution.py:36
  10.8 1.7 convert_multiply_fusion
  12.5 32.3 %all-to-all-done = bf16[2,1536,512]{2,1,0:T(8,128)(2,1)} async-done(((bf16[2,1536,512]{2,1,0:T(8,128)(2,1)}), bf16[2,1536,512]{2,1,0:T(8,128)(2,1)}, u32[]{:S(2)}, u32[]{:S(2)}) %all-to-all-start) | async-done | bytes 3145760 | tf_op jit(solution)/shard_map/all_to_all | solution.py:36
  44.8 27.6 %convolution_bitcast_fusion.2 = f32[6144,512]{0,1:T(8,128)} fusion(bf16[3072,512]{1,0:T(8,128)(2,1)} %bitcast, bf16[6144,3072]{1,0:T(8,128)(2,1)} %bitcast.26), kind=kOutput, calls=%fused_computation.2 | convolution fusion | flops 19327352832 | bytes 53477376 | tf_op jit(solution)/shard_map/dot_general | solution.py:33
  72.4 6.0 %slice_subtract_fusion.10 = (f32[1536,128]{0,1:T(8,128)S(1)}, f32[1536,128]{0,1:T(8,128)S(1)}, f32[1536,128]{0,1:T(8,128)S(1)}, f32[1536,128]{0,1:T(8,128)S(1)},...) fusion(f32[6144,512]{0,1:T(8,128)} %convolution_bitcast_fusion.2), kind=kLoop, calls=%fused_computation.49 | loop fusion | flops 1572864 | bytes 18874368 | tf_op jit(solution)/shard_map/sub | solution.py:16
  79.5 4.5 %collective-permute-start = (bf16[1536,256]{0,1:T(8,128)(2,1)S(1)}, bf16[1536,256]{0,1:T(8,128)(2,1)S(1)}, u32[]{:S(2)}, u32[]{:S(2)}) collective-permute-start(bf16[1536,256]{0,1:T(8,128)(2,1)S(1)} %get-tuple-element.33), channel_id=1, source_target_pairs={{0,2},{2,4},{4,6},{6,8},{8,10},{10,12},{12,14},{14,16},{16,18},{18... | collective-permute-start | bytes 2359304 | tf_op jit(solution)/shard_map/ppermute | solution.py:12
  84.0 1.9 collective-permute-start.1
  85.9 15.4 %collective-permute-done = bf16[1536,256]{0,1:T(8,128)(2,1)S(1)} collective-permute-done((bf16[1536,256]{0,1:T(8,128)(2,1)S(1)}, bf16[1536,256]{0,1:T(8,128)(2,1)S(1)}, u32[]{:S(2)}, u32[]{:S(2)}) %collective-permute-start) | collective-permute-done | bytes 786464 | tf_op jit(solution)/shard_map/ppermute | solution.py:12
  101.3 1.6 collective-permute-done.1
  103.3 34.4 %all_to_all.15 = bf16[2,1536,512]{1,2,0:T(8,128)(2,1)} all-to-all(bf16[2,1536,512]{1,2,0:T(8,128)(2,1)S(1)} %pad_maximum_fusion.1), channel_id=1, replica_groups=mesh['layer'=16,'row'=2] {'row'}, dimensions={0} | all-to-all | bytes 6291456 | tf_op jit(solution)/shard_map/all_to_all | solution.py:36
  137.8 4.7 %copy.8 = bf16[2,1536,512]{2,1,0:T(8,128)(2,1)} copy(bf16[2,1536,512]{1,2,0:T(8,128)(2,1)} %all_to_all.15) | data formatting | bytes 6291456 | tf_op jit(solution)/shard_map/all_to_all | solution.py:36
  142.5 27.6 %convolution_bitcast_fusion.1 = f32[6144,512]{0,1:T(8,128)} fusion(bf16[3072,512]{1,0:T(8,128)(2,1)} %bitcast.24, bf16[6144,3072]{1,0:T(8,128)(2,1)} %bitcast.27), kind=kOutput, calls=%fused_computation.1 | convolution fusion | flops 19327352832 | bytes 53477376 | tf_op jit(solution)/shard_map/dot_general | solution.py:33
  170.1 6.0 %slice_subtract_fusion.6 = (f32[1536,128]{0,1:T(8,128)S(1)}, f32[1536,128]{0,1:T(8,128)S(1)}, f32[1536,128]{0,1:T(8,128)S(1)}, f32[1536,128]{0,1:T(8,128)S(1)}, ...) fusion(f32[6144,512]{0,1:T(8,128)} %convolution_bitcast_fusion.1), kind=kLoop, calls=%fused_computation.41 | loop fusion | flops 1572864 | bytes 18874368 | tf_op jit(solution)/shard_map/sub | solution.py:16
  177.2 4.6 %collective-permute-start.2 = (bf16[1536,256]{0,1:T(8,128)(2,1)S(1)}, bf16[1536,256]{0,1:T(8,128)(2,1)S(1)}, u32[]{:S(2)}, u32[]{:S(2)}) collective-permute-start(bf16[1536,256]{0,1:T(8,128)(2,1)S(1)} %get-tuple-element.31), channel_id=1, source_target_pairs={{0,2},{2,4},{4,6},{6,8},{8,10},{10,12},{12,14},{14,16},{16,18},{18... | collective-permute-start | bytes 2359304 | tf_op jit(solution)/shard_map/ppermute | solution.py:12
  181.8 1.9 collective-permute-start.3
  183.8 15.4 %collective-permute-done.2 = bf16[1536,256]{0,1:T(8,128)(2,1)S(1)} collective-permute-done((bf16[1536,256]{0,1:T(8,128)(2,1)S(1)}, bf16[1536,256]{0,1:T(8,128)(2,1)S(1)}, u32[]{:S(2)}, u32[]{:S(2)}) %collective-permute-start.2) | collective-permute-done | bytes 786464 | tf_op jit(solution)/shard_map/ppermute | solution.py:12
  199.6 32.3 %all_to_all.16 = bf16[2,1536,512]{1,2,0:T(8,128)(2,1)} all-to-all(bf16[2,1536,512]{1,2,0:T(8,128)(2,1)S(1)} %pad_maximum_fusion.2), channel_id=1, replica_groups=mesh['layer'=16,'row'=2] {'row'}, dimensions={0} | all-to-all | bytes 6291456 | tf_op jit(solution)/shard_map/all_to_all | solution.py:36
  231.9 4.7 %copy.9 = bf16[2,1536,512]{2,1,0:T(8,128)(2,1)} copy(bf16[2,1536,512]{1,2,0:T(8,128)(2,1)} %all_to_all.16) | data formatting | bytes 6291456 | tf_op jit(solution)/shard_map/all_to_all | solution.py:36
  236.6 27.6 %convolution_bitcast_fusion = f32[6144,512]{0,1:T(8,128)} fusion(bf16[3072,512]{1,0:T(8,128)(2,1)} %bitcast.25, bf16[6144,3072]{1,0:T(8,128)(2,1)} %bitcast.28), kind=kOutput, calls=%fused_computation | convolution fusion | flops 19327352832 | bytes 53477376 | tf_op jit(solution)/shard_map/dot_general | solution.py:33
  264.2 6.0 %slice_subtract_fusion.2 = (f32[1536,128]{0,1:T(8,128)S(1)}, f32[1536,128]{0,1:T(8,128)S(1)}, f32[1536,128]{0,1:T(8,128)S(1)}, f32[1536,128]{0,1:T(8,128)S(1)}, ...) fusion(f32[6144,512]{0,1:T(8,128)} %convolution_bitcast_fusion), kind=kLoop, calls=%fused_computation.33 | loop fusion | flops 1572864 | bytes 18874368 | tf_op jit(solution)/shard_map/sub | solution.py:16
  271.3 4.6 %collective-permute-start.4 = (bf16[1536,256]{0,1:T(8,128)(2,1)S(1)}, bf16[1536,256]{0,1:T(8,128)(2,1)S(1)}, u32[]{:S(2)}, u32[]{:S(2)}) collective-permute-start(bf16[1536,256]{0,1:T(8,128)(2,1)S(1)} %get-tuple-element.29), channel_id=1, source_target_pairs={{0,2},{2,4},{4,6},{6,8},{8,10},{10,12},{12,14},{14,16},{16,18},{18... | collective-permute-start | bytes 2359304 | tf_op jit(solution)/shard_map/ppermute | solution.py:12
  275.9 1.9 collective-permute-start.5
  277.9 15.4 %collective-permute-done.4 = bf16[1536,256]{0,1:T(8,128)(2,1)S(1)} collective-permute-done((bf16[1536,256]{0,1:T(8,128)(2,1)S(1)}, bf16[1536,256]{0,1:T(8,128)(2,1)S(1)}, u32[]{:S(2)}, u32[]{:S(2)}) %collective-permute-start.4) | collective-permute-done | bytes 786464 | tf_op jit(solution)/shard_map/ppermute | solution.py:12
  (18 shorter events, 7.4 us)
Async XLA Ops:
  3.8 5.4 %copy-start = (bf16[1536,512]{1,0:T(8,128)(2,1)S(1)}, bf16[1536,512]{1,0:T(8,128)(2,1)}, u32[]{:S(2)}) copy-start(bf16[1536,512]{1,0:T(8,128)(2,1)} %param.6) | copy-start | bytes 4718596
  3.8 40.9 %all-to-all-start = ((bf16[2,1536,512]{2,1,0:T(8,128)(2,1)}), bf16[2,1536,512]{2,1,0:T(8,128)(2,1)}, u32[]{:S(2)}, u32[]{:S(2)}) async-start(bf16[2,1536,512]{2,1,0:T(8,128)(2,1)} %pad_maximum_fusion), calls=%async_computation | async-start | bytes 6291456 | tf_op jit(solution)/shard_map/all_to_all | solution.py:36
  9.2 1.6 copy-start.1
  79.5 21.9 %collective-permute-start = (bf16[1536,256]{0,1:T(8,128)(2,1)S(1)}, bf16[1536,256]{0,1:T(8,128)(2,1)S(1)}, u32[]{:S(2)}, u32[]{:S(2)}) collective-permute-start(bf16[1536,256]{0,1:T(8,128)(2,1)S(1)} %get-tuple-element.33), channel_id=1, source_target_pairs={{0,2},{2,4},{4,6},{6,8},{8,10},{10,12},{12,14},{14,16},{16,18},{18... | collective-permute-start | bytes 2359304 | tf_op jit(solution)/shard_map/ppermute | solution.py:12
  84.0 18.9 %collective-permute-start.1 = (bf16[1536,256]{0,1:T(8,128)(2,1)S(1)}, bf16[1536,256]{0,1:T(8,128)(2,1)S(1)}, u32[]{:S(2)}, u32[]{:S(2)}) collective-permute-start(bf16[1536,256]{0,1:T(8,128)(2,1)S(1)} %get-tuple-element.34), channel_id=1, source_target_pairs={{2,0},{4,2},{6,4},{8,6},{10,8},{12,10},{14,12},{16,14},{18,16},{20... | collective-permute-start | bytes 2359304 | tf_op jit(solution)/shard_map/ppermute | solution.py:12
  177.2 21.9 %collective-permute-start.2 = (bf16[1536,256]{0,1:T(8,128)(2,1)S(1)}, bf16[1536,256]{0,1:T(8,128)(2,1)S(1)}, u32[]{:S(2)}, u32[]{:S(2)}) collective-permute-start(bf16[1536,256]{0,1:T(8,128)(2,1)S(1)} %get-tuple-element.31), channel_id=1, source_target_pairs={{0,2},{2,4},{4,6},{6,8},{8,10},{10,12},{12,14},{14,16},{16,18},{18... | collective-permute-start | bytes 2359304 | tf_op jit(solution)/shard_map/ppermute | solution.py:12
  181.8 17.3 %collective-permute-start.3 = (bf16[1536,256]{0,1:T(8,128)(2,1)S(1)}, bf16[1536,256]{0,1:T(8,128)(2,1)S(1)}, u32[]{:S(2)}, u32[]{:S(2)}) collective-permute-start(bf16[1536,256]{0,1:T(8,128)(2,1)S(1)} %get-tuple-element.32), channel_id=1, source_target_pairs={{2,0},{4,2},{6,4},{8,6},{10,8},{12,10},{14,12},{16,14},{18,16},{20... | collective-permute-start | bytes 2359304 | tf_op jit(solution)/shard_map/ppermute | solution.py:12
  271.3 22.0 %collective-permute-start.4 = (bf16[1536,256]{0,1:T(8,128)(2,1)S(1)}, bf16[1536,256]{0,1:T(8,128)(2,1)S(1)}, u32[]{:S(2)}, u32[]{:S(2)}) collective-permute-start(bf16[1536,256]{0,1:T(8,128)(2,1)S(1)} %get-tuple-element.29), channel_id=1, source_target_pairs={{0,2},{2,4},{4,6},{6,8},{8,10},{10,12},{12,14},{14,16},{16,18},{18... | collective-permute-start | bytes 2359304 | tf_op jit(solution)/shard_map/ppermute | solution.py:12
  275.9 17.3 %collective-permute-start.5 = (bf16[1536,256]{0,1:T(8,128)(2,1)S(1)}, bf16[1536,256]{0,1:T(8,128)(2,1)S(1)}, u32[]{:S(2)}, u32[]{:S(2)}) collective-permute-start(bf16[1536,256]{0,1:T(8,128)(2,1)S(1)} %get-tuple-element.30), channel_id=1, source_target_pairs={{2,0},{4,2},{6,4},{8,6},{10,8},{12,10},{14,12},{16,14},{18,16},{20... | collective-permute-start | bytes 2359304 | tf_op jit(solution)/shard_map/ppermute | solution.py:12
